TPU v7x, 256 devices: a whole 4x4x8 slice. The times are simulated.
256 devices in a mesh: orow: 16 (over z_lo, x), ocol: 16 (over z_hi, y, core).
Axes of the slice: x: 4, y: 4, z: 8 (z_hi: 2, z_lo: 4; z = z_hi * 4 + z_lo), core: 2. Of those that a mesh axis runs over, the one named last changes fastest.
Arguments:
- amplitudes: bfloat16 [16, 16, 512, 512], P('orow', 'ocol'), may hold values from -6 to 6
- tile_mask: int32 [16, 16, 2, 2], P('orow', 'ocol'), may hold values 0 or 1
- domain_tiles: int32 [16, 16, 2], replicated, may hold values from 0 to 7, as said below
- cholesky: bfloat16 [16, 2048, 2048], P('ocol'), as said below
Outputs:
- ladder_sym: float32 [16, 16, 512, 512], P('orow', 'ocol')
Inputs may be any that keep to these rules, and one draw needn't show every extreme that they name: `domain_tiles`: for every pair the 2 tile numbers differ, and pair (j, i) lists the same tiles in the same order as pair (i, j). Every vector cholesky[q] is a symmetric 2048 x 2048 matrix.
All inputs are finite; a program needn't handle non-finite values. No bound on the sum of `tile_mask` on one device may be relied on, other than what follows from the above.
Results may differ from a plain program's by a relative error of at most 0.0029.
Values may be sent and summed in bfloat16 or wider, within the bound.
A program may use at most 128 MiB of HBM per device.

v0:
```python
import jax
import jax.numpy as jnp
from jax import lax
from jax.sharding import PartitionSpec as P

TILE = 256
K = 2


def pick_tiles(local_factor, chosen):
    number = local_factor.shape[0]
    tiles = local_factor.shape[1] // TILE
    blocked = local_factor.reshape(number, tiles, TILE, tiles, TILE)
    picked = blocked[:, chosen[..., :, None], :, chosen[..., None, :], :]
    leading = chosen.ndim - 1
    permuted = tuple(range(leading)) + (leading + 2, leading, leading + 3, leading + 1, leading + 4)
    width = chosen.shape[-1] * TILE
    return picked.transpose(permuted).reshape(chosen.shape[:-1] + (number, width, width))


def masked(amplitudes, tile_mask):
    row_pairs = amplitudes.shape[0]
    col_pairs = amplitudes.shape[1]
    shaped = amplitudes.reshape(row_pairs, col_pairs, K, TILE, K, TILE)
    weights = tile_mask.astype(jnp.bfloat16)[:, :, :, None, :, None]
    return (shaped * weights).reshape(amplitudes.shape)


def shards(amplitudes, tile_mask, domain_tiles, cholesky):
    row_pairs = amplitudes.shape[0]
    row_domains = lax.dynamic_slice_in_dim(
        domain_tiles, lax.axis_index("orow") * row_pairs, row_pairs, 0
    )
    weighted = masked(amplitudes, tile_mask)
    gathered = lax.all_gather(weighted, "ocol", axis=1, tiled=True)
    factor = pick_tiles(cholesky, row_domains)
    inner = jnp.einsum(
        "ijqac,ijcd->ijqad", factor, gathered, preferred_element_type=jnp.float32
    ).astype(jnp.bfloat16)
    summed = lax.psum_scatter(
        jnp.einsum("ijqad,ijqbd->jiab", inner, factor, preferred_element_type=jnp.float32),
        "ocol",
        scatter_dimension=0,
        tiled=True,
    )
    ladder = summed.transpose(1, 0, 2, 3)
    turned = lax.all_to_all(ladder, "ocol", split_axis=2, concat_axis=1, tiled=True)
    turned = lax.all_to_all(
        lax.all_to_all(turned, "orow", split_axis=1, concat_axis=0, tiled=True),
        "ocol",
        split_axis=0,
        concat_axis=2,
        tiled=True,
    )
    return ladder + turned.transpose(1, 0, 3, 2)


def solution(mesh):
    return jax.shard_map(
        shards,
        mesh=mesh,
        in_specs=(
            P("orow", "ocol", None, None),
            P("orow", "ocol", None, None),
            P(),
            P("ocol", None, None),
        ),
        out_specs=P("orow", "ocol", None, None),
        check_vma=False,
    )
```

profile of v0, /device:TPU:32, one launch (start us, length us, event | category | flops | bytes accessed | tf_op | source)
XLA Modules:
  0.0 467.5 jit_solution(741445048212051335)
XLA Ops:
  6.5 0.0 all-gather.2.cloned.1.call-start
  6.5 0.7 convert_bitcast_fusion
  7.2 0.3 mul.16
  7.6 0.3 mul.17
  7.9 1.9 bitcast_multiply_fusion
  9.8 0.0 all-gather.2.cloned.1.call-update
  9.8 0.0 reduce-scatter.2.cloned.1.call-start
  9.9 0.7 compare_select_fusion
  10.6 0.1 copy.29
  10.7 0.1 reshape.87
  10.8 10.3 %copy.40 = bf16[256,8,8,256]{3,2,1,0:T(8,128)(2,1)} copy(bf16[256,8,8,256]{3,1,2,0:T(8,128)(2,1)} %bitcast.45) | data formatting | bytes 16777216
  21.1 8.8 %copy.30 = bf16[8,256,8,256]{3,1,2,0:T(8,128)(2,1)} copy(bf16[8,256,8,256]{3,2,1,0:T(8,128)(2,1)} %bitcast.44) | data formatting | bytes 16777216 | tf_op jit(solution)/shard_map/reshape | solution.py:13
  29.9 9.4 %gather_fusion = bf16[64,256,256]{2,1,0:T(8,128)(2,1)} fusion(bf16[8,256,8,256]{3,1,2,0:T(8,128)(2,1)} %copy.30, s32[64]{0:T(128)S(1)} %reshape.87), kind=kCustom, calls=%fused_computation | custom fusion | bytes 16777728 | tf_op jit(solution)/shard_map/gather | solution.py:14
  39.4 16.3 %copy.31 = bf16[1,16,1,2,256,2,256]{6,5,4,3,1,2,0:T(2,128)(2,1)} copy(bf16[1,16,1,2,256,2,256]{6,4,5,3,1,2,0:T(8,128)(2,1)} %bitcast.43) | data formatting | bytes 16777216 | tf_op jit(solution)/shard_map/transpose | solution.py:18
  55.6 14.2 %reshape.81 = bf16[16,512,512]{2,1,0:T(8,128)(2,1)} reshape(bf16[1,16,1,2,256,2,256]{6,5,4,3,1,2,0:T(2,128)(2,1)} %copy.31) | data formatting | bytes 16777216 | tf_op jit(solution)/shard_map/reshape.10
  69.9 50.2 %all-gather.2.cloned.1.call-done = bf16[1,16,512,512]{3,2,0,1:T(8,128)(2,1)} async-done(((bf16[1,1,512,512]{3,2,0,1:T(8,128)(2,1)}), bf16[1,16,512,512]{3,2,0,1:T(8,128)(2,1)}) %all-gather.2.cloned.1.call-update) | async-done | bytes 8388624 | tf_op jit(solution)/shard_map/all_gather | solution.py:35
  120.1 22.0 %convolution_bitcast_fusion = f32[16,1,512,512]{3,2,0,1:T(8,128)} fusion(bf16[16,512,512]{2,1,0:T(8,128)(2,1)} %reshape.81, bf16[1,16,512,512]{3,2,0,1:T(8,128)(2,1)} %all-gather.2.cloned.1.call-done), kind=kOutput, calls=%fused_computation.1 | convolution fusion | flops 8594128896 | bytes 33554432 | tf_op jit(solution)/shard_map/ijqad,ijqbd->jiab/dot_general | solution.py:41
  142.0 0.0 reduce-scatter.2.cloned.1.call-update
  142.0 213.5 %reduce-scatter.2.cloned.1.call-done = f32[1,1,512,512]{3,2,0,1:T(8,128)} async-done(((f32[16,1,512,512]{3,2,0,1:T(8,128)}), f32[1,1,512,512]{3,2,0,1:T(8,128)}) %reduce-scatter.2.cloned.1.call-update) | async-done | bytes 1048592 | tf_op jit(solution)/shard_map/reduce_scatter | solution.py:40
  355.5 0.0 copy-start
  355.5 2.4 copy.33
  357.9 34.7 %all_to_all.36 = f32[1,1,512,512]{3,0,1,2:T(1,128)S(1)} all-to-all(f32[1,1,512,512]{3,0,1,2:T(1,128)S(1)} %copy.33), channel_id=1, replica_groups=mesh['orow'=16,'ocol'=16] {'ocol'}, dimensions={2} | all-to-all | bytes 2097152 | tf_op jit(solution)/shard_map/all_to_all | solution.py:47
  392.6 0.1 copy.34
  392.7 32.2 %all_to_all.37 = f32[1,16,32,512]{3,2,0,1:T(8,128)S(1)} all-to-all(f32[1,16,32,512]{3,2,0,1:T(8,128)S(1)} %copy.34), channel_id=1, replica_groups=mesh['orow'=16,'ocol'=16] {'orow'}, dimensions={1} | all-to-all | bytes 2097152 | tf_op jit(solution)/shard_map/all_to_all | solution.py:49
  424.9 34.2 %all_to_all.38 = f32[16,1,32,512]{3,2,1,0:T(8,128)S(1)} all-to-all(f32[16,1,32,512]{3,2,1,0:T(8,128)S(1)} %bitcast.47), channel_id=1, replica_groups=mesh['orow'=16,'ocol'=16] {'ocol'}, dimensions={0} | all-to-all | bytes 2097152 | tf_op jit(solution)/shard_map/all_to_all | solution.py:48
  459.1 0.3 copy.36
  459.5 0.0 copy-done
  459.5 1.2 fusion.7
  (5 shorter events, 0.0 us)
Async XLA Ops:
  6.5 113.5 %all-gather.2.cloned.1.call-start = ((), (), s32[]{:S(2)}) async-start(), calls=%async_computation.4 | async-start | bytes 8912896 | tf_op jit(solution)/shard_map/all_gather | solution.py:35
  9.8 345.7 %reduce-scatter.2.cloned.1.call-start = ((), (), s32[]{:S(2)}) async-start(), calls=%async_computation.5 | async-start | bytes 17825792 | tf_op jit(solution)/shard_map/reduce_scatter | solution.py:40
  355.5 103.9 %copy-start = (f32[1,1,512,512]{3,2,0,1:T(8,128)S(1)}, f32[1,1,512,512]{3,2,0,1:T(8,128)}, u32[]{:S(2)}) copy-start(f32[1,1,512,512]{3,2,0,1:T(8,128)} %reduce-scatter.2.cloned.1.call-done) | copy-start | bytes 3145732
Sparse Core Ops, SparseCore 0:
  10.1 109.9 all-gather.1
  142.2 213.3 reduce-scatter.1
where the time goes:
time: 468 us; the launch traced here: 467 us
  waiting for transfers between devices  264 us (56%)
  blocking collectives  101 us (22%)
  local copies, waits for them, and re-layouts  62.7 us (13%)
  matrix products  22 us (5%)
  between operations  13.5 us (3%)
    reduce_scatter x1, waiting for transfers between devices, shards(): lax.psum_scatter(jnp.einsum('ijqad,ijqbd->jiab', inner, factor, preferred...  213 us
    all_gather x1, waiting for transfers between devices, shards(): gathered = lax.all_gather(weighted, 'ocol', axis=1, tiled=True)  50.2 us
    all_to_all x1, blocking collectives, shards(): lax.all_to_all(ladder, 'ocol', split_axis=2, concat_axis=1, tiled=True)  34.7 us
    all_to_all x1, blocking collectives, shards(): lax.all_to_all(lax.all_to_all(turned, 'orow', split_axis=1, concat_axis=0...  34.2 us
    all_to_all x1, blocking collectives, shards(): lax.all_to_all(turned, 'orow', split_axis=1, concat_axis=0, tiled=True)  32.2 us
    dot_general x1, matrix products, shards(): jnp.einsum('ijqad,ijqbd->jiab', inner, factor, preferred_element_type=jnp...  22 us
    transpose x1, local copies, waits for them, and re-layouts, pick_tiles(): picked.transpose(permuted)  16.3 us
    another operation x1, local copies, waits for them, and re-layouts  14.2 us
  transfers between devices with their start and end apart: 2, of which 2 were waited for; matrix products, arithmetic and copies ran while one was open for 13% of the time, Pallas kernels for 0%

commit v1 on v0

--- a/solution.py
+++ b/solution.py
@@ -45,12 +45,20 @@
     )
     ladder = summed.transpose(1, 0, 2, 3)
     turned = lax.all_to_all(ladder, "ocol", split_axis=2, concat_axis=1, tiled=True)
-    turned = lax.all_to_all(
-        lax.all_to_all(turned, "orow", split_axis=1, concat_axis=0, tiled=True),
-        "ocol",
-        split_axis=0,
-        concat_axis=2,
-        tiled=True,
+    turned = jnp.concatenate(
+        lax.all_to_all(
+            jnp.stack(
+                jnp.split(
+                    lax.all_to_all(turned, "orow", split_axis=1, concat_axis=0, tiled=True),
+                    lax.axis_size("ocol"),
+                    axis=0,
+                )
+            ),
+            "ocol",
+            0,
+            0,
+        ),
+        axis=2,
     )
     return ladder + turned.transpose(1, 0, 3, 2)
 

time: 468 us -> 468 us (level)
    unnamed x3 -> x18, local copies, waits for them, and re-layouts: 10.3 us -> 10.4 us
    another operation x1 -> x2, local copies, waits for them, and re-layouts: 14.2 us -> 14.2 us
where the time goes in v1:
time: 468 us
  waiting for transfers between devices  264 us (56%)
  blocking collectives  101 us (22%)
  local copies, waits for them, and re-layouts  62.9 us (13%)
  matrix products  22 us (5%)
  between operations  13.6 us (3%)
    reduce_scatter x1, waiting for transfers between devices, shards(): lax.psum_scatter(jnp.einsum('ijqad,ijqbd->jiab', inner, factor, preferred...  213 us
    all_gather x1, waiting for transfers between devices, shards(): gathered = lax.all_gather(weighted, 'ocol', axis=1, tiled=True)  50.2 us
    all_to_all x1, blocking collectives, shards(): lax.all_to_all(ladder, 'ocol', split_axis=2, concat_axis=1, tiled=True)  34.7 us
    all_to_all x1, blocking collectives, shards(): lax.all_to_all(jnp.stack(jnp.split(lax.all_to_all(turned, 'orow', split_a...  34.2 us
    all_to_all x1, blocking collectives, shards(): lax.all_to_all(turned, 'orow', split_axis=1, concat_axis=0, tiled=True)  32.2 us
    dot_general x1, matrix products, shards(): jnp.einsum('ijqad,ijqbd->jiab', inner, factor, preferred_element_type=jnp...  22 us
    transpose x1, local copies, waits for them, and re-layouts, pick_tiles(): picked.transpose(permuted)  16.3 us
    another operation x1, local copies, waits for them, and re-layouts  14.2 us
  transfers between devices with their start and end apart: 2, of which 2 were waited for; matrix products, arithmetic and copies ran while one was open for 13% of the time, Pallas kernels for 0%

profile of v1, /device:TPU:32, one launch (start us, length us, event | category | flops | bytes accessed | tf_op | source)
XLA Modules:
  0.0 467.7 jit_solution(5482543911931519086)
XLA Ops:
  6.5 0.0 all-gather.2.cloned.1.call-start
  6.5 0.7 convert_bitcast_fusion
  7.2 0.3 mul.16
  7.6 0.3 mul.17
  7.9 1.9 bitcast_multiply_fusion
  9.8 0.0 all-gather.2.cloned.1.call-update
  9.8 0.0 reduce-scatter.2.cloned.1.call-start
  9.9 0.7 compare_select_fusion
  10.6 0.1 copy.87
  10.7 0.1 reshape.120
  10.8 10.3 %copy.111 = bf16[256,8,8,256]{3,2,1,0:T(8,128)(2,1)} copy(bf16[256,8,8,256]{3,1,2,0:T(8,128)(2,1)} %bitcast.117) | data formatting | bytes 16777216
  21.1 8.8 %copy.88 = bf16[8,256,8,256]{3,1,2,0:T(8,128)(2,1)} copy(bf16[8,256,8,256]{3,2,1,0:T(8,128)(2,1)} %bitcast.116) | data formatting | bytes 16777216 | tf_op jit(solution)/shard_map/reshape | solution.py:13
  29.9 9.4 %gather_fusion = bf16[64,256,256]{2,1,0:T(8,128)(2,1)} fusion(bf16[8,256,8,256]{3,1,2,0:T(8,128)(2,1)} %copy.88, s32[64]{0:T(128)S(1)} %reshape.120), kind=kCustom, calls=%fused_computation | custom fusion | bytes 16777728 | tf_op jit(solution)/shard_map/gather | solution.py:14
  39.4 16.3 %copy.89 = bf16[1,16,1,2,256,2,256]{6,5,4,3,1,2,0:T(2,128)(2,1)} copy(bf16[1,16,1,2,256,2,256]{6,4,5,3,1,2,0:T(8,128)(2,1)} %bitcast.115) | data formatting | bytes 16777216 | tf_op jit(solution)/shard_map/transpose | solution.py:18
  55.6 14.2 %reshape.113 = bf16[16,512,512]{2,1,0:T(8,128)(2,1)} reshape(bf16[1,16,1,2,256,2,256]{6,5,4,3,1,2,0:T(2,128)(2,1)} %copy.89) | data formatting | bytes 16777216 | tf_op jit(solution)/shard_map/reshape.11
  69.9 50.2 %all-gather.2.cloned.1.call-done = bf16[1,16,512,512]{3,2,0,1:T(8,128)(2,1)} async-done(((bf16[1,1,512,512]{3,2,0,1:T(8,128)(2,1)}), bf16[1,16,512,512]{3,2,0,1:T(8,128)(2,1)}) %all-gather.2.cloned.1.call-update) | async-done | bytes 8388624 | tf_op jit(solution)/shard_map/all_gather | solution.py:35
  120.1 22.0 %convolution_bitcast_fusion = f32[16,1,512,512]{3,2,0,1:T(8,128)} fusion(bf16[16,512,512]{2,1,0:T(8,128)(2,1)} %reshape.113, bf16[1,16,512,512]{3,2,0,1:T(8,128)(2,1)} %all-gather.2.cloned.1.call-done), kind=kOutput, calls=%fused_computation.1 | convolution fusion | flops 8594128896 | bytes 33554432 | tf_op jit(solution)/shard_map/ijqad,ijqbd->jiab/dot_general | solution.py:41
  142.0 0.0 reduce-scatter.2.cloned.1.call-update
  142.0 213.5 %reduce-scatter.2.cloned.1.call-done = f32[1,1,512,512]{3,2,0,1:T(8,128)} async-done(((f32[16,1,512,512]{3,2,0,1:T(8,128)}), f32[1,1,512,512]{3,2,0,1:T(8,128)}) %reduce-scatter.2.cloned.1.call-update) | async-done | bytes 1048592 | tf_op jit(solution)/shard_map/reduce_scatter | solution.py:40
  355.5 0.0 copy-start
  355.5 2.4 copy.91
  357.9 34.7 %all_to_all.29 = f32[1,1,512,512]{3,0,1,2:T(1,128)S(1)} all-to-all(f32[1,1,512,512]{3,0,1,2:T(1,128)S(1)} %copy.91), channel_id=1, replica_groups=mesh['orow'=16,'ocol'=16] {'ocol'}, dimensions={2} | all-to-all | bytes 2097152 | tf_op jit(solution)/shard_map/all_to_all | solution.py:47
  392.6 0.1 copy.92
  392.7 32.2 %all_to_all.30 = f32[1,16,32,512]{3,2,0,1:T(8,128)S(1)} all-to-all(f32[1,16,32,512]{3,2,0,1:T(8,128)S(1)} %copy.92), channel_id=1, replica_groups=mesh['orow'=16,'ocol'=16] {'orow'}, dimensions={1} | all-to-all | bytes 2097152 | tf_op jit(solution)/shard_map/all_to_all | solution.py:52
  425.1 34.2 %all_to_all.31 = f32[16,1,1,32,512]{4,3,2,1,0:T(8,128)S(1)} all-to-all(f32[16,1,1,32,512]{4,3,2,1,0:T(8,128)S(1)} %fusion.8), channel_id=1, replica_groups=mesh['orow'=16,'ocol'=16] {'ocol'}, dimensions={0} | all-to-all | bytes 2097152 | tf_op jit(solution)/shard_map/all_to_all | solution.py:49
  459.4 0.3 copy.107
  459.7 0.0 copy-done
  459.7 1.2 fusion.7
  (21 shorter events, 0.1 us)
Async XLA Ops:
  6.5 113.5 %all-gather.2.cloned.1.call-start = ((), (), s32[]{:S(2)}) async-start(), calls=%async_computation.4 | async-start | bytes 8912896 | tf_op jit(solution)/shard_map/all_gather | solution.py:35
  9.8 345.7 %reduce-scatter.2.cloned.1.call-start = ((), (), s32[]{:S(2)}) async-start(), calls=%async_computation.5 | async-start | bytes 17825792 | tf_op jit(solution)/shard_map/reduce_scatter | solution.py:40
  355.5 104.2 %copy-start = (f32[1,1,512,512]{3,2,0,1:T(8,128)S(1)}, f32[1,1,512,512]{3,2,0,1:T(8,128)}, u32[]{:S(2)}) copy-start(f32[1,1,512,512]{3,2,0,1:T(8,128)} %reduce-scatter.2.cloned.1.call-done) | copy-start | bytes 3145732
Sparse Core Ops, SparseCore 0:
  10.1 109.9 all-gather.1
  142.2 213.3 reduce-scatter.1
